TPU v7x, 128 devices: a whole 4x4x4 slice. The times are simulated.
128 devices in a mesh: row: 4 (over y), col: 32 (over z, x, core).
Axes of the slice: x: 4, y: 4, z: 4, core: 2. Of those that a mesh axis runs over, the one named last changes fastest.
Arguments:
- rhs: float32 [16384, 256], P(('row', 'col')), may hold values from -6 to 6
- dense: float32 [2, 16384, 16384], P(None, 'col', 'row'), may hold values from -0.03125 to 0.03125
- inflow: float32 [128, 2, 2, 512, 256], P(('row', 'col')), may hold values from -0.25 to 0.25
- robin: float32 [128, 2, 2, 512, 512], P(('row', 'col')), may hold values from -0.1875 to 0.1875
- outflow: float32 [128, 2, 256, 1024], P(('row', 'col')), may hold values from -0.0390625 to 0.0390625
- trace_row: int32 [32, 128, 8], replicated, may hold values from 0 to 511
- trace_count: int32 [32, 128], replicated, may hold values from 0 to 8, as said below
- current_row: int32 [128, 128, 2], replicated, may hold values from 0 to 127
- current_count: int32 [128, 128], replicated, may hold values from 0 to 2, as said below
Outputs:
- solution: float32 [16384, 256], P(('row', 'col'))
Inputs may be any that keep to these rules, and one draw needn't show every extreme that they name: `trace_row`: repeats may occur. `trace_count`: 8 is reached, and some subdomain takes 8 from every block. `current_row`: repeats may occur. `current_count`: some subdomain gives 2 to every block, and some block receives 2 from every subdomain.
All inputs are finite; a program needn't handle non-finite values.
Results may differ from a plain program's by a relative error of at most 0.0001.
Values sent between devices are 32-bit elements; how exact they have to be, the bound alone decides.
A program may use at most 128 MiB of HBM per device.

v0:
```python
import jax
import jax.numpy as jnp
from jax import lax
from jax.sharding import PartitionSpec as P

ITERS = 2
EPS = 1e-06
SCALE = 2.0 ** (-24)
HIGH = lax.Precision.HIGH


def extended(x, sides, width):
    for axis, dim in sides:
        size, length = (lax.axis_size(axis), x.shape[dim])
        up = [(i, (i + 1) % size) for i in range(size - 1)]
        down = [(j, i) for i, j in up]
        last = lax.slice_in_dim(x, length - width, length, axis=dim)
        leading = lax.slice_in_dim(x, 0, width, axis=dim)
        before = lax.ppermute(last, axis, up)
        after = lax.ppermute(leading, axis, down)
        x = jnp.concatenate([before, x, after], axis=dim)
    return x


def combine(real_half, imag_half, waves):
    return jnp.concatenate(
        [
            real_half[..., :waves] - imag_half[..., waves:],
            real_half[..., waves:] + imag_half[..., :waves],
        ],
        axis=-1,
    )


def scale_vector(vector, coef, waves):
    real_part = vector[:, :waves]
    imag_part = vector[:, waves:]
    return jnp.concatenate(
        [coef[0] * real_part - coef[1] * imag_part, coef[0] * imag_part + coef[1] * real_part],
        axis=1,
    )


def inner_terms(left, right, waves):
    left_real, left_imag = (left[:, :waves], left[:, waves:])
    right_real, right_imag = (right[:, :waves], right[:, waves:])
    return (
        jnp.sum(left_real * right_real + left_imag * right_imag, axis=0),
        jnp.sum(left_real * right_imag - left_imag * right_real, axis=0),
    )


def square_terms(vector, waves):
    halves = jnp.sum(vector * vector, axis=0)
    return halves[:waves] + halves[waves:]


def cmul(first, second):
    return (
        first[0] * second[0] - first[1] * second[1],
        first[0] * second[1] + first[1] * second[0],
    )


def cconj(first):
    return (first[0], -first[1])


def csub(first, second):
    return (first[0] - second[0], first[1] - second[1])


def cadd(first, second):
    return (first[0] + second[0], first[1] + second[1])


def cdiv(first, second):
    denom = second[0] * second[0] + second[1] * second[1]
    numer = cmul(first, cconj(second))
    return (numer[0] / denom, numer[1] / denom)


def solve_small(gram, target):
    size = len(target)
    gram = [list(line) for line in gram]
    target = list(target)
    for pivot in range(size):
        for lower in range(pivot + 1, size):
            factor = cdiv(gram[lower][pivot], gram[pivot][pivot])
            for other in range(pivot, size):
                gram[lower][other] = csub(gram[lower][other], cmul(factor, gram[pivot][other]))
            target[lower] = csub(target[lower], cmul(factor, target[pivot]))
    result = [None] * size
    for pivot in reversed(range(size)):
        summed = target[pivot]
        for other in range(pivot + 1, size):
            summed = csub(summed, cmul(gram[pivot][other], result[other]))
        result[pivot] = cdiv(summed, gram[pivot][pivot])
    return result


def least_squares(hess, beta, steps):
    zero_pair = (jnp.zeros_like(beta), jnp.zeros_like(beta))
    gram = []
    for first in range(steps):
        line = []
        for second in range(steps):
            summed = zero_pair
            for height in range(steps + 1):
                summed = cadd(
                    summed,
                    cmul(
                        cconj(hess.get((height, first), zero_pair)),
                        hess.get((height, second), zero_pair),
                    ),
                )
            line.append(summed)
        gram.append(line)
    target = [
        cmul(cconj(hess.get((0, first), zero_pair)), (beta, jnp.zeros_like(beta)))
        for first in range(steps)
    ]
    return solve_small(gram, target)


def turned(vector, waves):
    return jnp.concatenate([-vector[..., waves:], vector[..., :waves]], axis=-1)


def conj_mul(first, second):
    return cmul(cconj(first), second)


def krylov_coefficients(sums):
    norm0, p_real, p_imag, norm1, t_real, t_imag, s_real, s_imag, norm2 = sums
    zero = jnp.zeros_like(norm0)
    beta2 = norm0 + EPS
    beta = jnp.sqrt(beta2)
    unit = norm0 / beta2
    lack = EPS / beta2
    p = (p_real / beta2, p_imag / beta2)
    q = norm1 / beta2
    back = 1.0 / SCALE
    t = (t_real / beta2 * back, t_imag / beta2 * back)
    s = (s_real / beta2 * back, s_imag / beta2 * back)
    z = norm2 / beta2 * back * back
    p_abs = p[0] * p[0] + p[1] * p[1]
    h00 = (unit + p[0], p[1])
    h10 = jnp.sqrt(unit * lack + 2.0 * lack * p[0] + (q - p_abs) + EPS)
    a = 1.0 / h10
    g = (lack - p[0], -p[1])
    g_abs = g[0] * g[0] + g[1] * g[1]
    gp = cmul(g, p)
    h01 = (a * (lack * h00[0] + (t[0] + gp[0])), a * (lack * h00[1] + (t[1] + gp[1])))
    short = a * a * (lack * (1.0 - lack) * (unit + 2.0 * p[0]) + lack * p_abs + EPS)
    length = 1.0 - short
    gt = conj_mul(g, t)
    m = (
        a * a * (s[0] + g[0] * q + gt[0] + g_abs * p[0]),
        a * a * (s[1] + g[1] * q + gt[1] + g_abs * p[1]),
    )
    spread = a * a * (z + 2.0 * conj_mul(g, s)[0] + g_abs * q)
    h11 = (length + m[0], m[1])
    remain = length * short + 2.0 * short * m[0] + (spread - m[0] * m[0] - m[1] * m[1])
    remain = remain - h01[0] * h01[0] - h01[1] * h01[1]
    h21 = jnp.sqrt(remain + EPS)
    hess = {(0, 0): h00, (1, 0): (h10, zero), (0, 1): h01, (1, 1): h11, (2, 1): (h21, zero)}
    y0, y1 = least_squares(hess, beta, ITERS)
    ya = (y1[0] * a, y1[1] * a)
    yg = cmul(ya, g)
    return (((y0[0] + yg[0]) / beta, (y0[1] + yg[1]) / beta), (ya[0] / beta, ya[1] / beta))


def on_device(
    rhs, dense, inflow, robin, outflow, trace_row, trace_count, current_row, current_count
):
    n_row = lax.axis_size("row")
    n_col = lax.axis_size("col")
    devices = n_row * n_col
    row_at = lax.axis_index("row")
    col_at = lax.axis_index("col")
    device_at = row_at * n_col + col_at
    block_rows, lanes = rhs.shape
    waves = lanes // 2
    tpair = trace_row.shape[2]
    tback = current_row.shape[2]
    inflow_mine = inflow[0]
    robin_mine = robin[0]
    outflow_mine = outflow[0]
    trace_rows = lax.dynamic_index_in_dim(trace_row, col_at, 0, keepdims=False)
    trace_live = lax.dynamic_index_in_dim(trace_count, col_at, 0, keepdims=False)
    trace_keep = (jnp.arange(tpair, dtype=jnp.int32)[None, :] < trace_live[:, None]).astype(
        jnp.float32
    )
    basis = [rhs]
    for step in range(ITERS):
        operate_vector = basis[step] if step == 0 else basis[step] * SCALE
        piece = lax.all_gather(operate_vector, "col", axis=0, tiled=True)
        real_cols = dense[0]
        imag_cols = dense[1]
        field = jnp.dot(real_cols, piece, precision=HIGH, preferred_element_type=jnp.float32)
        field = field + jnp.dot(
            imag_cols, turned(piece, waves), precision=HIGH, preferred_element_type=jnp.float32
        )
        buffer = (
            jnp.take(field, trace_rows.reshape(-1), axis=0).reshape(devices, tpair, lanes)
            * trace_keep[:, :, None]
        )
        arrived = lax.all_to_all(buffer, ("row", "col"), split_axis=0, concat_axis=0, tiled=True)
        slots = jnp.sum(arrived.reshape(n_row, n_col, tpair, lanes), axis=0)
        slots = slots.reshape(n_col * tpair, lanes)
        mixed = jnp.einsum("fpmk,kl->fpml", inflow_mine, slots, precision=HIGH)
        excite = combine(mixed[:, 0], mixed[:, 1], waves)
        mixed = jnp.einsum("fpmn,fnl->fpml", robin_mine, excite, precision=HIGH)
        local = combine(mixed[:, 0], mixed[:, 1], waves)
        padded = extended(local, ((("row", "col"), 0),), 1)
        near = jnp.stack([padded[0], padded[3]], axis=0)
        mixed = jnp.einsum("fpmn,fnl->fpml", robin_mine, near, precision=HIGH)
        faces = local + combine(mixed[:, 0], mixed[:, 1], waves)
        flat = faces.reshape(faces.shape[0] * faces.shape[1], lanes)
        mixed = jnp.einsum("pkn,nl->pkl", outflow_mine, flat, precision=HIGH)
        currents = combine(mixed[0], mixed[1], waves)
        operate_arrived = lax.all_to_all(
            currents.reshape(devices, tback, lanes),
            ("row", "col"),
            split_axis=0,
            concat_axis=0,
            tiled=True,
        )
        own_rows = lax.dynamic_index_in_dim(current_row, device_at, 0, keepdims=False)
        own_live = lax.dynamic_index_in_dim(current_count, device_at, 0, keepdims=False)
        alive = (jnp.arange(tback, dtype=jnp.int32)[None, :] < own_live[:, None]).astype(
            jnp.float32
        )
        landed = (
            jnp.zeros((block_rows, lanes), jnp.float32)
            .at[own_rows.reshape(-1)]
            .add((operate_arrived * alive[..., None]).reshape(-1, lanes))
        )
        basis.append(landed)
    u0, b0, b1 = basis
    sums = [square_terms(u0, waves), *inner_terms(u0, b0, waves), square_terms(b0, waves)]
    sums += [*inner_terms(u0, b1, waves), *inner_terms(b0, b1, waves), square_terms(b1, waves)]
    sums = lax.psum(jnp.stack(sums, axis=0), ("row", "col"))
    first, second = krylov_coefficients([sums[i] for i in range(9)])
    return scale_vector(u0, first, waves) + scale_vector(b0, second, waves)


def solution(mesh):
    placed = (
        P(("row", "col"), None),
        P(None, "col", "row"),
        P(("row", "col"), None, None, None, None),
        P(("row", "col"), None, None, None, None),
        P(("row", "col"), None, None, None),
        P(),
        P(),
        P(),
        P(),
    )
    return jax.shard_map(
        on_device, mesh=mesh, in_specs=placed, out_specs=P(("row", "col"), None), check_vma=False
    )
```

profile of v0, /device:TPU:1, one launch (start us, length us, event | category | flops | bytes accessed | tf_op | source)
XLA Modules:
  0.0 399.5 jit_solution(4154344122775271763)
XLA Ops:
  6.5 0.7 all-gather.3.cloned.1.call-update
  7.3 0.7 constant_dynamic-slice_fusion.2
  8.2 0.7 fusion.115
  9.0 50.4 %all-gather.3.cloned.1.call-done = f32[4096,256]{1,0:T(8,128)} async-done(((f32[128,256]{1,0:T(8,128)}), f32[4096,256]{1,0:T(8,128)}) %all-gather.3.cloned.1.call-update) | async-done | bytes 4194320 | tf_op jit(solution)/shard_map/all_gather | solution.py:198
  59.4 2.6 slice_negate_fusion.1
  62.0 7.8 %fusion.6 = f32[512,256]{1,0:T(8,128)S(1)} fusion(f32[4096,256]{1,0:T(8,128)} %all-gather.3.cloned.1.call-done, f32[2,512,4096]{2,1,0:T(8,128)} %param.12), kind=kOutput, calls=%fused_computation.10 | convolution fusion | flops 3221225472 | bytes 13107200 | tf_op jit(solution)/shard_map/dot_general | solution.py:201
  69.8 0.2 copy-done.3
  70.1 3.6 fusion.63
  73.7 4.7 %gather_fusion = f32[1024,256]{1,0:T(8,128)} fusion(f32[512,256]{1,0:T(8,128)S(1)} %fusion.63, s32[1024]{0:T(1024)S(1)} %fusion.110), kind=kCustom, calls=%fused_computation.clone | custom fusion | bytes 2101248 | tf_op jit(solution)/shard_map/jit(_take)/gather | solution.py:206
  78.4 1.6 bitcast_multiply_fusion.1
  79.9 26.8 %all_to_all.20 = f32[128,8,256]{2,1,0:T(8,128)S(1)} all-to-all(f32[128,8,256]{2,1,0:T(8,128)S(1)} %bitcast_multiply_fusion.1), channel_id=1, replica_groups=mesh['row'=4,'col'=32] {'row','col'}, dimensions={0} | all-to-all | bytes 2097152 | tf_op jit(solution)/shard_map/all_to_all | solution.py:209
  106.8 1.9 fusion.46
  108.9 0.2 slice_subtract_fusion.5
  109.1 1.8 copy-done.1
  110.9 2.2 fusion.34
  113.3 0.2 slice_subtract_fusion.4
  113.5 1.0 fusion.101
  114.5 3.0 collective-permute-start
  117.5 2.1 collective-permute-start.1
  119.7 0.7 constant_dynamic-slice_fusion.3
  120.6 1.0 copy.26
  121.8 2.1 collective-permute-done
  124.0 4.4 %collective-permute-done.1 = f32[1,512,256]{1,2,0:T(8,128)} collective-permute-done((f32[1,512,256]{1,2,0:T(8,128)}, f32[1,512,256]{1,2,0:T(8,128)}, u32[]{:S(2)}, u32[]{:S(2)}) %collective-permute-start.1) | collective-permute-done | bytes 524320 | tf_op jit(solution)/shard_map/ppermute | solution.py:20
  128.4 4.4 %fusion.37 = f32[2,2,512,256]{2,3,1,0:T(8,128)S(1)} fusion(f32[1,2,2,512,512]{4,3,2,1,0:T(8,128)} %param.14, f32[1,512,256]{1,2,0:T(8,128)} %collective-permute-done.1, f32[1,512,256]{1,2,0:T(8,128)} %collective-permute-done), kind=kOutput, calls=%fused_computation.41 | convolution fusion | flops 1610874880 | bytes 7340032 | tf_op jit(solution)/shard_map/fpmn,fnl->fpml/dot_general | solution.py:218
  133.0 1.2 slice_subtract_fusion.3
  134.2 2.0 copy.29
  136.2 2.0 copy.30
  138.3 3.8 fusion.52
  142.3 0.8 reshape.140
  143.2 11.1 %all-to-all-start.1 = ((f32[128,2,256]{2,1,0:T(2,128)}), f32[128,2,256]{2,1,0:T(2,128)S(1)}, u32[]{:S(2)}, u32[]{:S(2)}) async-start(f32[128,2,256]{2,1,0:T(2,128)} %reshape.140), calls=%async_computation.1 | async-start | bytes 524288 | tf_op jit(solution)/shard_map/all_to_all | solution.py:223
  154.3 0.2 all-gather.5.cloned.1.call-start
  154.5 0.7 fusion.116
  155.3 10.0 %all-to-all-done.1 = f32[128,2,256]{2,1,0:T(2,128)S(1)} async-done(((f32[128,2,256]{2,1,0:T(2,128)}), f32[128,2,256]{2,1,0:T(2,128)S(1)}, u32[]{:S(2)}, u32[]{:S(2)}) %all-to-all-start.1) | async-done | bytes 262176 | tf_op jit(solution)/shard_map/all_to_all | solution.py:223
  165.7 2.0 scatter_custom_fusion
  167.7 0.7 multiply_reduce_fusion.1
  168.4 42.9 %all-gather.5.cloned.1.call-done = f32[4096,256]{1,0:T(8,128)} async-done(((f32[128,256]{1,0:T(8,128)}), f32[4096,256]{1,0:T(8,128)}) %all-gather.5.cloned.1.call-update) | async-done | bytes 4194320 | tf_op jit(solution)/shard_map/all_gather | solution.py:198
  211.3 11.5 %fusion.4 = f32[256,512]{1,0:T(8,128)S(1)} fusion(f32[4096,256]{1,0:T(8,128)} %all-gather.5.cloned.1.call-done, f32[2,512,4096]{2,1,0:T(8,128)} %param.12), kind=kOutput, calls=%fused_computation.8 | convolution fusion | flops 3221225472 | bytes 13107200 | tf_op jit(solution)/shard_map/dot_general | solution.py:201
  222.8 0.3 slice_negate_fusion
  223.1 9.6 %fusion.73 = f32[512,256]{0,1:T(8,128)S(1)} fusion(f32[256,512]{1,0:T(8,128)S(1)} %fusion.4, f32[2,512,4096]{2,1,0:T(8,128)} %param.12, f32[4096,128]{1,0:T(8,128)S(1)} %get-tuple-element.44, f32[4096,128]{1,0:T(8,128)S(1)} %get-tuple-element.43), kind=kOutput, calls=%fused_computation.51 | convolution fusion | flops 3222405120 | bytes 13631488 | tf_op jit(solution)/shard_map/dot_general | solution.py:202
  232.8 4.7 %gather_fusion.1 = f32[1024,256]{1,0:T(8,128)} fusion(f32[512,256]{1,0:T(8,128)S(1)} %copy.33, s32[1024]{0:T(1024)S(1)} %fusion.110), kind=kCustom, calls=%fused_computation.1.clone | custom fusion | bytes 2101248 | tf_op jit(solution)/shard_map/jit(_take)/gather | solution.py:206
  237.5 1.6 bitcast_multiply_fusion
  239.1 26.5 %all_to_all.21 = f32[128,8,256]{2,1,0:T(8,128)S(1)} all-to-all(f32[128,8,256]{2,1,0:T(8,128)S(1)} %bitcast_multiply_fusion), channel_id=1, replica_groups=mesh['row'=4,'col'=32] {'row','col'}, dimensions={0} | all-to-all | bytes 2097152 | tf_op jit(solution)/shard_map/all_to_all | solution.py:209
  265.5 0.8 reduce_sum.104
  266.3 2.8 fusion.49
  269.3 0.2 slice_subtract_fusion.2
  269.6 1.8 copy-done.2
  271.3 2.2 fusion.40
  274.0 1.0 fusion.100
  275.0 3.0 collective-permute-start.2
  278.0 2.1 collective-permute-start.3
  280.2 1.0 copy.37
  281.4 3.1 collective-permute-done.2
  284.4 4.4 %collective-permute-done.3 = f32[1,512,256]{1,2,0:T(8,128)} collective-permute-done((f32[1,512,256]{1,2,0:T(8,128)}, f32[1,512,256]{1,2,0:T(8,128)}, u32[]{:S(2)}, u32[]{:S(2)}) %collective-permute-start.3) | collective-permute-done | bytes 524320 | tf_op jit(solution)/shard_map/ppermute | solution.py:20
  288.8 4.4 %fusion.43 = f32[2,2,512,256]{2,3,1,0:T(8,128)S(1)} fusion(f32[1,2,2,512,512]{4,3,2,1,0:T(8,128)} %param.14, f32[1,512,256]{1,2,0:T(8,128)} %collective-permute-done.3, f32[1,512,256]{1,2,0:T(8,128)} %collective-permute-done.2), kind=kOutput, calls=%fused_computation.43 | convolution fusion | flops 1610874880 | bytes 7340032 | tf_op jit(solution)/shard_map/fpmn,fnl->fpml/dot_general | solution.py:218
  293.5 1.2 slice_subtract_fusion
  294.7 2.0 copy.40
  296.7 2.0 copy.41
  298.8 3.8 fusion.55
  302.8 0.8 reshape.145
  303.6 11.5 %all-to-all-start.3 = ((f32[128,2,256]{2,1,0:T(2,128)}), f32[128,2,256]{2,1,0:T(2,128)S(1)}, u32[]{:S(2)}, u32[]{:S(2)}) async-start(f32[128,2,256]{2,1,0:T(2,128)} %reshape.145), calls=%async_computation.3 | async-start | bytes 524288 | tf_op jit(solution)/shard_map/all_to_all | solution.py:223
  315.1 10.8 %all-to-all-done.3 = f32[128,2,256]{2,1,0:T(2,128)S(1)} async-done(((f32[128,2,256]{2,1,0:T(2,128)}), f32[128,2,256]{2,1,0:T(2,128)S(1)}, u32[]{:S(2)}, u32[]{:S(2)}) %all-to-all-start.3) | async-done | bytes 262176 | tf_op jit(solution)/shard_map/all_to_all | solution.py:223
  326.3 2.0 scatter_custom_fusion.1
  328.5 63.0 %psum.7 = f32[9,128]{1,0:T(8,128)S(1)} all-reduce(f32[9,128]{1,0:T(8,128)S(1)} %stack.47), channel_id=1, replica_groups=mesh['row'=4,'col'=32] {'row','col'}, use_global_device_ids=true, to_apply=%region_13.15 | all-reduce | flops 1152 | bytes 9216 | tf_op jit(solution)/shard_map/psum | solution.py:244
  391.7 0.7 maximum_add_fusion.2
  (60 shorter events, 4.1 us)
Async XLA Ops:
  6.5 100.3 %copy-start = (f32[1,2,2,512,256]{4,3,2,1,0:T(8,128)S(1)}, f32[1,2,2,512,256]{4,3,2,1,0:T(8,128)}, u32[]{:S(2)}) copy-start(f32[1,2,2,512,256]{4,3,2,1,0:T(8,128)} %param.13) | copy-start | bytes 6291460
  6.5 52.8 %all-gather.3.cloned.1.call-start = ((), (), s32[]{:S(2)}) async-start(), calls=%async_computation.4 | async-start | bytes 4325376 | tf_op jit(solution)/shard_map/all_gather | solution.py:198
  59.4 10.7 %copy-start.3 = (f32[2,512,4096]{2,1,0:T(8,128)S(1)}, f32[2,512,4096]{2,1,0:T(8,128)}, u32[]{:S(2)}) copy-start(f32[2,512,4096]{2,1,0:T(8,128)} %param.12) | copy-start | bytes 50331652
  108.7 2.2 copy-start.1
  114.5 9.4 %collective-permute-start = (f32[1,512,256]{1,2,0:T(8,128)}, f32[1,512,256]{1,2,0:T(8,128)}, u32[]{:S(2)}, u32[]{:S(2)}) collective-permute-start(f32[1,512,256]{1,2,0:T(8,128)} %get-tuple-element.73), channel_id=1, source_target_pairs={{0,1},{1,2},{2,3},{3,4},{4,5},{5,6},{6,7},{7,8},{8,9},{9,10},{10,1... | collective-permute-start | bytes 1572872 | tf_op jit(solution)/shard_map/ppermute | solution.py:19
  117.5 10.8 %collective-permute-start.1 = (f32[1,512,256]{1,2,0:T(8,128)}, f32[1,512,256]{1,2,0:T(8,128)}, u32[]{:S(2)}, u32[]{:S(2)}) collective-permute-start(f32[1,512,256]{1,2,0:T(8,128)} %get-tuple-element.74), channel_id=1, source_target_pairs={{1,0},{2,1},{3,2},{4,3},{5,4},{6,5},{7,6},{8,7},{9,8},{10,9},{11,1... | collective-permute-start | bytes 1572872 | tf_op jit(solution)/shard_map/ppermute | solution.py:20
  133.0 5.3 %copy-start.5 = (f32[2,512,128]{2,1,0:T(8,128)S(1)}, f32[2,512,128]{2,1,0:T(8,128)}, u32[]{:S(2)}) copy-start(f32[2,512,128]{2,1,0:T(8,128)} %copy.26) | copy-start | bytes 1572868
  143.2 22.1 %all-to-all-start.1 = ((f32[128,2,256]{2,1,0:T(2,128)}), f32[128,2,256]{2,1,0:T(2,128)S(1)}, u32[]{:S(2)}, u32[]{:S(2)}) async-start(f32[128,2,256]{2,1,0:T(2,128)} %reshape.140), calls=%async_computation.1 | async-start | bytes 524288 | tf_op jit(solution)/shard_map/all_to_all | solution.py:223
  154.3 57.0 %all-gather.5.cloned.1.call-start = ((), (), s32[]{:S(2)}) async-start(), calls=%async_computation.5 | async-start | bytes 4325376 | tf_op jit(solution)/shard_map/all_gather | solution.py:198
  211.3 11.5 %copy-start.4 = (f32[4096,256]{1,0:T(8,128)S(1)}, f32[4096,256]{1,0:T(8,128)}, u32[]{:S(2)}) copy-start(f32[4096,256]{1,0:T(8,128)} %all-gather.5.cloned.1.call-done) | copy-start | bytes 12582916
  269.1 2.2 copy-start.2
  273.7 6.4 %copy-start.7 = (f32[128,256]{1,0:T(8,128)S(1)}, f32[128,256]{1,0:T(8,128)}, u32[]{:S(2)}) copy-start(f32[128,256]{1,0:T(8,128)} %param.11) | copy-start | bytes 393220
  275.0 9.4 %collective-permute-start.2 = (f32[1,512,256]{1,2,0:T(8,128)}, f32[1,512,256]{1,2,0:T(8,128)}, u32[]{:S(2)}, u32[]{:S(2)}) collective-permute-start(f32[1,512,256]{1,2,0:T(8,128)} %get-tuple-element.71), channel_id=1, source_target_pairs={{0,1},{1,2},{2,3},{3,4},{4,5},{5,6},{6,7},{7,8},{8,9},{9,10},{10,1... | collective-permute-start | bytes 1572872 | tf_op jit(solution)/shard_map/ppermute | solution.py:19
  278.0 10.8 %collective-permute-start.3 = (f32[1,512,256]{1,2,0:T(8,128)}, f32[1,512,256]{1,2,0:T(8,128)}, u32[]{:S(2)}, u32[]{:S(2)}) collective-permute-start(f32[1,512,256]{1,2,0:T(8,128)} %get-tuple-element.72), channel_id=1, source_target_pairs={{1,0},{2,1},{3,2},{4,3},{5,4},{6,5},{7,6},{8,7},{9,8},{10,9},{11,1... | collective-permute-start | bytes 1572872 | tf_op jit(solution)/shard_map/ppermute | solution.py:20
  293.4 5.3 %copy-start.6 = (f32[2,512,128]{2,1,0:T(8,128)S(1)}, f32[2,512,128]{2,1,0:T(8,128)}, u32[]{:S(2)}) copy-start(f32[2,512,128]{2,1,0:T(8,128)} %copy.37) | copy-start | bytes 1572868
  303.6 22.3 %all-to-all-start.3 = ((f32[128,2,256]{2,1,0:T(2,128)}), f32[128,2,256]{2,1,0:T(2,128)S(1)}, u32[]{:S(2)}, u32[]{:S(2)}) async-start(f32[128,2,256]{2,1,0:T(2,128)} %reshape.145), calls=%async_computation.3 | async-start | bytes 524288 | tf_op jit(solution)/shard_map/all_to_all | solution.py:223
Sparse Core Ops, SparseCore 0:
  9.6 49.7 all-gather.2
  168.5 42.7 all-gather.4
where the time goes:
time: 406 us; the launch traced here: 399 us
  waiting for transfers between devices  129 us (32%)
  blocking collectives  116 us (29%)
  matrix products  58 us (14%)
  starting transfers between devices  33 us (8%)
  local copies, waits for them, and re-layouts  30.6 us (8%)
  other arithmetic  18.5 us (5%)
  between operations  14.2 us (3%)
    all_gather x2, waiting for transfers between devices, on_device(): piece = lax.all_gather(operate_vector, 'col', axis=0, tiled=True)  93.3 us
    psum x1, blocking collectives, on_device(): sums = lax.psum(jnp.stack(sums, axis=0), ('row', 'col'))  63 us
    all_to_all x2, blocking collectives, on_device(): lax.all_to_all(buffer, ('row', 'col'), split_axis=0, concat_axis=0, tiled...  53.2 us
    all_to_all x2, starting transfers between devices, on_device(): lax.all_to_all(currents.reshape(devices, tback, lanes), ('row', 'col'), s...  22.6 us
    all_to_all x2, waiting for transfers between devices, on_device(): lax.all_to_all(currents.reshape(devices, tback, lanes), ('row', 'col'), s...  20.8 us
    dot_general x2, matrix products, on_device(): jnp.dot(real_cols, piece, precision=HIGH, preferred_element_type=jnp.floa...  19.3 us
    dot_general x2, matrix products, on_device(): jnp.dot(imag_cols, turned(piece, waves), precision=HIGH, preferred_elemen...  13.2 us
    gather x2, local copies, waits for them, and re-layouts, on_device(): jnp.take(field, trace_rows.reshape(-1), axis=0)  9.36 us
  transfers between devices with their start and end apart: 8, of which 8 were waited for; matrix products, arithmetic and copies ran while one was open for 1% of the time, Pallas kernels for 0%

commit v1 on v0

--- a/solution.py
+++ b/solution.py
@@ -241,7 +241,7 @@
     u0, b0, b1 = basis
     sums = [square_terms(u0, waves), *inner_terms(u0, b0, waves), square_terms(b0, waves)]
     sums += [*inner_terms(u0, b1, waves), *inner_terms(b0, b1, waves), square_terms(b1, waves)]
-    sums = lax.psum(jnp.stack(sums, axis=0), ("row", "col"))
+    sums = jnp.sum(lax.all_gather(jnp.stack(sums, axis=0), ("row", "col")), axis=0)
     first, second = krylov_coefficients([sums[i] for i in range(9)])
     return scale_vector(u0, first, waves) + scale_vector(b0, second, waves)
 

time: 406 us -> 378 us (0.931)
  blocking collectives: 116 us -> 88.1 us
    psum x1 -> x0, blocking collectives: 63 us -> none  [on_device(): sums = lax.psum(jnp.stack(sums, axis=0), ('row', 'col'))]
    all_gather x0 -> x1, blocking collectives: none -> 34.9 us  [on_device(): lax.all_gather(jnp.stack(sums, axis=0), ('row', 'col'))]
  transfers between devices with their start and end apart: 8 -> 8, of which waited for: 8 -> 8; matrix products, arithmetic and copies ran while one was open for 1% -> 2% of each run, Pallas kernels for 0% -> 0%
where the time goes in v1:
time: 378 us; the launch traced here: 371 us
  waiting for transfers between devices  129 us (34%)
  blocking collectives  88.1 us (23%)
  matrix products  58 us (15%)
  starting transfers between devices  33 us (9%)
  local copies, waits for them, and re-layouts  30.6 us (8%)
  other arithmetic  18.7 us (5%)
  between operations  14.2 us (4%)
    all_gather x2, waiting for transfers between devices, on_device(): piece = lax.all_gather(operate_vector, 'col', axis=0, tiled=True)  93.3 us
    all_to_all x2, blocking collectives, on_device(): lax.all_to_all(buffer, ('row', 'col'), split_axis=0, concat_axis=0, tiled...  53.2 us
    all_gather x1, blocking collectives, on_device(): lax.all_gather(jnp.stack(sums, axis=0), ('row', 'col'))  34.9 us
    all_to_all x2, starting transfers between devices, on_device(): lax.all_to_all(currents.reshape(devices, tback, lanes), ('row', 'col'), s...  22.6 us
    all_to_all x2, waiting for transfers between devices, on_device(): lax.all_to_all(currents.reshape(devices, tback, lanes), ('row', 'col'), s...  20.8 us
    dot_general x2, matrix products, on_device(): jnp.dot(real_cols, piece, precision=HIGH, preferred_element_type=jnp.floa...  19.3 us
    dot_general x2, matrix products, on_device(): jnp.dot(imag_cols, turned(piece, waves), precision=HIGH, preferred_elemen...  13.2 us
    gather x2, local copies, waits for them, and re-layouts, on_device(): jnp.take(field, trace_rows.reshape(-1), axis=0)  9.36 us
  transfers between devices with their start and end apart: 8, of which 8 were waited for; matrix products, arithmetic and copies ran while one was open for 2% of the time, Pallas kernels for 0%

profile of v1, /device:TPU:1, one launch (start us, length us, event | category | flops | bytes accessed | tf_op | source)
XLA Modules:
  0.0 371.5 jit_solution(12982489129436301150)
XLA Ops:
  6.5 0.7 all-gather.5.cloned.1.call-update
  7.3 0.7 constant_dynamic-slice_fusion.2
  8.2 0.7 fusion.115
  9.0 50.4 %all-gather.5.cloned.1.call-done = f32[4096,256]{1,0:T(8,128)} async-done(((f32[128,256]{1,0:T(8,128)}), f32[4096,256]{1,0:T(8,128)}) %all-gather.5.cloned.1.call-update) | async-done | bytes 4194320 | tf_op jit(solution)/shard_map/all_gather | solution.py:198
  59.4 2.6 slice_negate_fusion.1
  62.0 7.8 %fusion.6 = f32[512,256]{1,0:T(8,128)S(1)} fusion(f32[4096,256]{1,0:T(8,128)} %all-gather.5.cloned.1.call-done, f32[2,512,4096]{2,1,0:T(8,128)} %param.12), kind=kOutput, calls=%fused_computation.10 | convolution fusion | flops 3221225472 | bytes 13107200 | tf_op jit(solution)/shard_map/dot_general | solution.py:201
  69.8 0.2 copy-done.3
  70.1 3.6 fusion.63
  73.7 4.7 %gather_fusion = f32[1024,256]{1,0:T(8,128)} fusion(f32[512,256]{1,0:T(8,128)S(1)} %fusion.63, s32[1024]{0:T(1024)S(1)} %fusion.110), kind=kCustom, calls=%fused_computation.clone | custom fusion | bytes 2101248 | tf_op jit(solution)/shard_map/jit(_take)/gather | solution.py:206
  78.4 1.6 bitcast_multiply_fusion.1
  79.9 26.8 %all_to_all.20 = f32[128,8,256]{2,1,0:T(8,128)S(1)} all-to-all(f32[128,8,256]{2,1,0:T(8,128)S(1)} %bitcast_multiply_fusion.1), channel_id=1, replica_groups=mesh['row'=4,'col'=32] {'row','col'}, dimensions={0} | all-to-all | bytes 2097152 | tf_op jit(solution)/shard_map/all_to_all | solution.py:209
  106.8 1.9 fusion.46
  108.9 0.2 slice_subtract_fusion.5
  109.1 1.8 copy-done.1
  110.9 2.2 fusion.34
  113.3 0.2 slice_subtract_fusion.4
  113.5 1.0 fusion.101
  114.5 3.0 collective-permute-start
  117.5 2.1 collective-permute-start.1
  119.7 0.7 constant_dynamic-slice_fusion.3
  120.6 1.0 copy.50
  121.8 2.1 collective-permute-done
  124.0 4.4 %collective-permute-done.1 = f32[1,512,256]{1,2,0:T(8,128)} collective-permute-done((f32[1,512,256]{1,2,0:T(8,128)}, f32[1,512,256]{1,2,0:T(8,128)}, u32[]{:S(2)}, u32[]{:S(2)}) %collective-permute-start.1) | collective-permute-done | bytes 524320 | tf_op jit(solution)/shard_map/ppermute | solution.py:20
  128.4 4.4 %fusion.37 = f32[2,2,512,256]{2,3,1,0:T(8,128)S(1)} fusion(f32[1,2,2,512,512]{4,3,2,1,0:T(8,128)} %param.14, f32[1,512,256]{1,2,0:T(8,128)} %collective-permute-done.1, f32[1,512,256]{1,2,0:T(8,128)} %collective-permute-done), kind=kOutput, calls=%fused_computation.41 | convolution fusion | flops 1610874880 | bytes 7340032 | tf_op jit(solution)/shard_map/fpmn,fnl->fpml/dot_general | solution.py:218
  133.0 1.2 slice_subtract_fusion.3
  134.2 2.0 copy.53
  136.2 2.0 copy.54
  138.3 3.8 %fusion.52 = f32[2,256,256]{1,2,0:T(8,128)S(1)} fusion(f32[1,2,256,1024]{3,2,1,0:T(8,128)} %param.15, f32[1024,128]{1,0:T(8,128)S(1)} %bitcast.201, f32[1024,128]{1,0:T(8,128)S(1)} %bitcast.199, f32[1024,128]{1,0:T(8,128)} %bitcast.205, f32[1024,128]{1,0:T(8,128)} %bitcast.203), kind=kOutput, calls=%fused_computation.46 | convolution fusion | flops 806092800 | bytes 4718592 | tf_op jit(solution)/shard_map/pkn,nl->pkl/dot_general | solution.py:221
  142.3 0.8 reshape.140
  143.2 11.1 %all-to-all-start.1 = ((f32[128,2,256]{2,1,0:T(2,128)}), f32[128,2,256]{2,1,0:T(2,128)S(1)}, u32[]{:S(2)}, u32[]{:S(2)}) async-start(f32[128,2,256]{2,1,0:T(2,128)} %reshape.140), calls=%async_computation.1 | async-start | bytes 524288 | tf_op jit(solution)/shard_map/all_to_all | solution.py:223
  154.3 0.2 all-gather.7.cloned.1.call-start
  154.5 0.7 fusion.116
  155.3 10.0 %all-to-all-done.1 = f32[128,2,256]{2,1,0:T(2,128)S(1)} async-done(((f32[128,2,256]{2,1,0:T(2,128)}), f32[128,2,256]{2,1,0:T(2,128)S(1)}, u32[]{:S(2)}, u32[]{:S(2)}) %all-to-all-start.1) | async-done | bytes 262176 | tf_op jit(solution)/shard_map/all_to_all | solution.py:223
  165.7 2.0 scatter_custom_fusion
  167.7 0.7 multiply_reduce_fusion.1
  168.4 42.9 %all-gather.7.cloned.1.call-done = f32[4096,256]{1,0:T(8,128)} async-done(((f32[128,256]{1,0:T(8,128)}), f32[4096,256]{1,0:T(8,128)}) %all-gather.7.cloned.1.call-update) | async-done | bytes 4194320 | tf_op jit(solution)/shard_map/all_gather | solution.py:198
  211.3 11.5 %fusion.4 = f32[256,512]{1,0:T(8,128)S(1)} fusion(f32[4096,256]{1,0:T(8,128)} %all-gather.7.cloned.1.call-done, f32[2,512,4096]{2,1,0:T(8,128)} %param.12), kind=kOutput, calls=%fused_computation.8 | convolution fusion | flops 3221225472 | bytes 13107200 | tf_op jit(solution)/shard_map/dot_general | solution.py:201
  222.8 0.3 slice_negate_fusion
  223.1 9.6 %fusion.73 = f32[512,256]{0,1:T(8,128)S(1)} fusion(f32[256,512]{1,0:T(8,128)S(1)} %fusion.4, f32[2,512,4096]{2,1,0:T(8,128)} %param.12, f32[4096,128]{1,0:T(8,128)S(1)} %get-tuple-element.44, f32[4096,128]{1,0:T(8,128)S(1)} %get-tuple-element.43), kind=kOutput, calls=%fused_computation.51 | convolution fusion | flops 3222405120 | bytes 13631488 | tf_op jit(solution)/shard_map/dot_general | solution.py:202
  232.8 4.7 %gather_fusion.1 = f32[1024,256]{1,0:T(8,128)} fusion(f32[512,256]{1,0:T(8,128)S(1)} %copy.57, s32[1024]{0:T(1024)S(1)} %fusion.110), kind=kCustom, calls=%fused_computation.1.clone | custom fusion | bytes 2101248 | tf_op jit(solution)/shard_map/jit(_take)/gather | solution.py:206
  237.5 1.6 bitcast_multiply_fusion
  239.1 26.5 %all_to_all.21 = f32[128,8,256]{2,1,0:T(8,128)S(1)} all-to-all(f32[128,8,256]{2,1,0:T(8,128)S(1)} %bitcast_multiply_fusion), channel_id=1, replica_groups=mesh['row'=4,'col'=32] {'row','col'}, dimensions={0} | all-to-all | bytes 2097152 | tf_op jit(solution)/shard_map/all_to_all | solution.py:209
  265.5 0.8 reduce_sum.113
  266.3 2.8 fusion.49
  269.3 0.2 slice_subtract_fusion.2
  269.6 1.8 copy-done.2
  271.3 2.2 fusion.40
  274.0 1.0 fusion.100
  275.0 3.0 collective-permute-start.2
  278.0 2.1 collective-permute-start.3
  280.2 1.0 copy.61
  281.4 3.1 collective-permute-done.2
  284.4 4.4 %collective-permute-done.3 = f32[1,512,256]{1,2,0:T(8,128)} collective-permute-done((f32[1,512,256]{1,2,0:T(8,128)}, f32[1,512,256]{1,2,0:T(8,128)}, u32[]{:S(2)}, u32[]{:S(2)}) %collective-permute-start.3) | collective-permute-done | bytes 524320 | tf_op jit(solution)/shard_map/ppermute | solution.py:20
  288.8 4.4 %fusion.43 = f32[2,2,512,256]{2,3,1,0:T(8,128)S(1)} fusion(f32[1,2,2,512,512]{4,3,2,1,0:T(8,128)} %param.14, f32[1,512,256]{1,2,0:T(8,128)} %collective-permute-done.3, f32[1,512,256]{1,2,0:T(8,128)} %collective-permute-done.2), kind=kOutput, calls=%fused_computation.43 | convolution fusion | flops 1610874880 | bytes 7340032 | tf_op jit(solution)/shard_map/fpmn,fnl->fpml/dot_general | solution.py:218
  293.5 1.2 slice_subtract_fusion
  294.7 2.0 copy.64
  296.7 2.0 copy.65
  298.8 3.8 %fusion.55 = f32[2,256,256]{1,2,0:T(8,128)S(1)} fusion(f32[1,2,256,1024]{3,2,1,0:T(8,128)} %param.15, f32[1024,128]{1,0:T(8,128)S(1)} %bitcast.202, f32[1024,128]{1,0:T(8,128)S(1)} %bitcast.200, f32[1024,128]{1,0:T(8,128)} %bitcast.206, f32[1024,128]{1,0:T(8,128)} %bitcast.204), kind=kOutput, calls=%fused_computation.47 | convolution fusion | flops 806092800 | bytes 4718592 | tf_op jit(solution)/shard_map/pkn,nl->pkl/dot_general | solution.py:221
  302.8 0.8 reshape.145
  303.6 11.5 %all-to-all-start.3 = ((f32[128,2,256]{2,1,0:T(2,128)}), f32[128,2,256]{2,1,0:T(2,128)S(1)}, u32[]{:S(2)}, u32[]{:S(2)}) async-start(f32[128,2,256]{2,1,0:T(2,128)} %reshape.145), calls=%async_computation.3 | async-start | bytes 524288 | tf_op jit(solution)/shard_map/all_to_all | solution.py:223
  315.1 10.8 %all-to-all-done.3 = f32[128,2,256]{2,1,0:T(2,128)S(1)} async-done(((f32[128,2,256]{2,1,0:T(2,128)}), f32[128,2,256]{2,1,0:T(2,128)S(1)}, u32[]{:S(2)}, u32[]{:S(2)}) %all-to-all-start.3) | async-done | bytes 262176 | tf_op jit(solution)/shard_map/all_to_all | solution.py:223
  326.3 2.0 scatter_custom_fusion.1
  328.5 34.9 %all-gather.1 = f32[128,9,128]{2,1,0:T(8,128)S(1)} all-gather(f32[1,9,128]{2,1,0:T(8,128)S(1)} %bitcast.207), channel_id=2, replica_groups=mesh['row'=4,'col'=32] {'row','col'}, dimensions={0}, use_global_device_ids=true | all-gather | bytes 594432 | tf_op jit(solution)/shard_map/all_gather | solution.py:244
  363.7 0.7 maximum_add_fusion.2
  (61 shorter events, 4.3 us)
Async XLA Ops:
  6.5 100.3 %copy-start = (f32[1,2,2,512,256]{4,3,2,1,0:T(8,128)S(1)}, f32[1,2,2,512,256]{4,3,2,1,0:T(8,128)}, u32[]{:S(2)}) copy-start(f32[1,2,2,512,256]{4,3,2,1,0:T(8,128)} %param.13) | copy-start | bytes 6291460
  6.5 52.8 %all-gather.5.cloned.1.call-start = ((), (), s32[]{:S(2)}) async-start(), calls=%async_computation.4 | async-start | bytes 4325376 | tf_op jit(solution)/shard_map/all_gather | solution.py:198
  59.4 10.7 %copy-start.3 = (f32[2,512,4096]{2,1,0:T(8,128)S(1)}, f32[2,512,4096]{2,1,0:T(8,128)}, u32[]{:S(2)}) copy-start(f32[2,512,4096]{2,1,0:T(8,128)} %param.12) | copy-start | bytes 50331652
  108.7 2.2 copy-start.1
  114.5 9.4 %collective-permute-start = (f32[1,512,256]{1,2,0:T(8,128)}, f32[1,512,256]{1,2,0:T(8,128)}, u32[]{:S(2)}, u32[]{:S(2)}) collective-permute-start(f32[1,512,256]{1,2,0:T(8,128)} %get-tuple-element.73), channel_id=1, source_target_pairs={{0,1},{1,2},{2,3},{3,4},{4,5},{5,6},{6,7},{7,8},{8,9},{9,10},{10,1... | collective-permute-start | bytes 1572872 | tf_op jit(solution)/shard_map/ppermute | solution.py:19
  117.5 10.8 %collective-permute-start.1 = (f32[1,512,256]{1,2,0:T(8,128)}, f32[1,512,256]{1,2,0:T(8,128)}, u32[]{:S(2)}, u32[]{:S(2)}) collective-permute-start(f32[1,512,256]{1,2,0:T(8,128)} %get-tuple-element.74), channel_id=1, source_target_pairs={{1,0},{2,1},{3,2},{4,3},{5,4},{6,5},{7,6},{8,7},{9,8},{10,9},{11,1... | collective-permute-start | bytes 1572872 | tf_op jit(solution)/shard_map/ppermute | solution.py:20
  133.0 5.3 %copy-start.5 = (f32[2,512,128]{2,1,0:T(8,128)S(1)}, f32[2,512,128]{2,1,0:T(8,128)}, u32[]{:S(2)}) copy-start(f32[2,512,128]{2,1,0:T(8,128)} %copy.50) | copy-start | bytes 1572868
  143.2 22.1 %all-to-all-start.1 = ((f32[128,2,256]{2,1,0:T(2,128)}), f32[128,2,256]{2,1,0:T(2,128)S(1)}, u32[]{:S(2)}, u32[]{:S(2)}) async-start(f32[128,2,256]{2,1,0:T(2,128)} %reshape.140), calls=%async_computation.1 | async-start | bytes 524288 | tf_op jit(solution)/shard_map/all_to_all | solution.py:223
  154.3 57.0 %all-gather.7.cloned.1.call-start = ((), (), s32[]{:S(2)}) async-start(), calls=%async_computation.5 | async-start | bytes 4325376 | tf_op jit(solution)/shard_map/all_gather | solution.py:198
  211.3 11.5 %copy-start.4 = (f32[4096,256]{1,0:T(8,128)S(1)}, f32[4096,256]{1,0:T(8,128)}, u32[]{:S(2)}) copy-start(f32[4096,256]{1,0:T(8,128)} %all-gather.7.cloned.1.call-done) | copy-start | bytes 12582916
  269.1 2.2 copy-start.2
  273.7 6.4 %copy-start.7 = (f32[128,256]{1,0:T(8,128)S(1)}, f32[128,256]{1,0:T(8,128)}, u32[]{:S(2)}) copy-start(f32[128,256]{1,0:T(8,128)} %param.11) | copy-start | bytes 393220
  275.0 9.4 %collective-permute-start.2 = (f32[1,512,256]{1,2,0:T(8,128)}, f32[1,512,256]{1,2,0:T(8,128)}, u32[]{:S(2)}, u32[]{:S(2)}) collective-permute-start(f32[1,512,256]{1,2,0:T(8,128)} %get-tuple-element.71), channel_id=1, source_target_pairs={{0,1},{1,2},{2,3},{3,4},{4,5},{5,6},{6,7},{7,8},{8,9},{9,10},{10,1... | collective-permute-start | bytes 1572872 | tf_op jit(solution)/shard_map/ppermute | solution.py:19
  278.0 10.8 %collective-permute-start.3 = (f32[1,512,256]{1,2,0:T(8,128)}, f32[1,512,256]{1,2,0:T(8,128)}, u32[]{:S(2)}, u32[]{:S(2)}) collective-permute-start(f32[1,512,256]{1,2,0:T(8,128)} %get-tuple-element.72), channel_id=1, source_target_pairs={{1,0},{2,1},{3,2},{4,3},{5,4},{6,5},{7,6},{8,7},{9,8},{10,9},{11,1... | collective-permute-start | bytes 1572872 | tf_op jit(solution)/shard_map/ppermute | solution.py:20
  293.4 5.3 %copy-start.6 = (f32[2,512,128]{2,1,0:T(8,128)S(1)}, f32[2,512,128]{2,1,0:T(8,128)}, u32[]{:S(2)}) copy-start(f32[2,512,128]{2,1,0:T(8,128)} %copy.61) | copy-start | bytes 1572868
  303.6 22.3 %all-to-all-start.3 = ((f32[128,2,256]{2,1,0:T(2,128)}), f32[128,2,256]{2,1,0:T(2,128)S(1)}, u32[]{:S(2)}, u32[]{:S(2)}) async-start(f32[128,2,256]{2,1,0:T(2,128)} %reshape.145), calls=%async_computation.3 | async-start | bytes 524288 | tf_op jit(solution)/shard_map/all_to_all | solution.py:223
Sparse Core Ops, SparseCore 0:
  9.6 49.7 all-gather.4
  168.5 42.7 all-gather.6
